TPU v7x, 256 devices: a whole 4x4x8 slice. The times are simulated.
256 devices in a mesh: dp: 32 (over z, x_hi, core), row: 4 (over y), col: 2 (over x_lo).
Axes of the slice: x: 4 (x_hi: 2, x_lo: 2; x = x_hi * 2 + x_lo), y: 4, z: 8, core: 2. Of those that a mesh axis runs over, the one named last changes fastest.
Arguments:
- tokens: bfloat16 [6144, 4096], P('dp', ('row', 'col')), may hold values from -6 to 6
- in_weight: bfloat16 [4096, 3, 4096], P('dp', None, ('row', 'col')), may hold values from -0.09375 to 0.09375
- short_filter: float32 [3, 3, 4096], P(None, None, ('row', 'col')), may hold values from -3 to 3
- long_filter: bfloat16 [256, 128], P(('row', 'col')), may hold values from -0.59765625 to 0.59765625
- grad_out: bfloat16 [6144, 4096], P('dp', ('row', 'col')), may hold values from -6 to 6
Outputs:
- mixed: bfloat16 [6144, 4096], P('dp', ('row', 'col'))
- grad_in: bfloat16 [6144, 4096], P('dp', ('row', 'col'))
- grad_weight: float32 [4096, 3, 4096], P('dp', None, ('row', 'col'))
- grad_long: float32 [256, 128], P(('row', 'col'))
- grad_short: float32 [3, 3, 4096], P(None, None, ('row', 'col'))
All inputs are finite; a program needn't handle non-finite values.
Results may differ from a plain program's by a relative error of at most 0.019.
Values may be sent and summed in bfloat16 or wider, within the bound.
A program may use at most 128 MiB of HBM per device.

v0:
```python
import jax
import jax.numpy as jnp
from jax import lax
from jax.sharding import PartitionSpec as P


def from_behind(block, axis, distance):
    devices = range(lax.axis_size(axis))
    route = [(i - distance, i) for i in devices if i - distance in devices]
    return lax.ppermute(block, axis, route)


def toeplitz(leading, rows, span):
    groups = leading.shape[0]
    width = rows + span
    seed_row = jnp.concatenate(
        [leading, jnp.zeros((groups, width - leading.shape[1]), leading.dtype)], axis=1
    )
    tiled = jnp.tile(seed_row, (1, rows))
    skewed = tiled[:, : rows * (width - 1)].reshape(groups, rows, width - 1)
    return skewed[:, :, :span]


def to_groups(values, ngroups, members):
    count = values.shape[0]
    return values.reshape(count, ngroups, members).transpose(1, 2, 0)


def from_groups(values):
    groups, members, count = values.shape
    return values.transpose(2, 0, 1).reshape(count, groups * members)


def per_device(tokens, in_weight, short_filter, long_filter, grad_out):
    rows = tokens.shape[0]
    local = grad_out.shape[1]
    nshort = short_filter.shape[0]
    ntaps = long_filter.shape[1]
    ngroups = long_filter.shape[0]
    members = local // ngroups
    margin = ntaps - 1
    span = rows + margin
    scale = float(rows * lax.axis_size("dp")) ** (-0.5)
    whole = lax.all_gather(tokens, ("row", "col"), axis=1, tiled=True)
    full_w = lax.all_gather(in_weight, "dp", axis=0, tiled=True)
    mixed_in = jnp.einsum("sd,dic->sic", whole, full_w, preferred_element_type=jnp.float32).astype(
        jnp.bfloat16
    )
    before = from_behind(mixed_in[rows - margin - nshort + 1 :], "dp", 1)
    extended = jnp.concatenate([before, mixed_in], axis=0).astype(jnp.float32)
    long_feats = jnp.zeros((span, 3, local), jnp.float32)
    for j in range(nshort):
        long_feats = (
            long_feats + short_filter[j][None] * extended[nshort - 1 - j : nshort - 1 - j + span]
        )
    product_ext = (long_feats[:, 1] * long_feats[:, 2]).astype(jnp.bfloat16)
    feats = long_feats[margin:]
    short_rows = extended[margin:]
    product_cols = to_groups(product_ext, ngroups, members)
    causal = toeplitz(long_filter[:, ::-1], rows, span)
    conv = from_groups(
        jnp.einsum("gst,gct->gcs", causal, product_cols, preferred_element_type=jnp.float32)
    )
    mixed = (feats[:, 0] * conv).astype(jnp.bfloat16)
    upstream = grad_out.astype(jnp.float32)
    grad_query = upstream * conv
    grad_conv = (upstream * feats[:, 0]).astype(jnp.bfloat16)
    after = from_behind(grad_conv[:margin], "dp", -1)
    grad_ext = jnp.concatenate([grad_conv, after], axis=0)
    anti = toeplitz(long_filter, rows, span)
    grad_product = from_groups(
        jnp.einsum(
            "gst,gct->gcs",
            anti,
            to_groups(grad_ext, ngroups, members),
            preferred_element_type=jnp.float32,
        )
    )
    reversed_cols = jnp.concatenate(
        [product_cols[:, :, ::-1], jnp.zeros((ngroups, members, rows), product_cols.dtype)], axis=2
    )
    width = span + rows
    pairs = jnp.einsum(
        "gcs,gcu->gsu",
        to_groups(grad_conv, ngroups, members),
        reversed_cols,
        preferred_element_type=jnp.float32,
    )
    diagonal = pairs.reshape(ngroups, rows * width)[:, : rows * (width - 1)].reshape(
        ngroups, rows, width - 1
    )
    filter_part = jnp.sum(diagonal[:, :, rows - 1 : rows - 1 + ntaps], axis=1)
    grad_feats = jnp.stack(
        [grad_query, grad_product * feats[:, 2], grad_product * feats[:, 1]], axis=1
    )
    later = from_behind(grad_feats[: nshort - 1], "dp", -1)
    feats_ext = jnp.concatenate([grad_feats, later], axis=0)
    grad_acc = jnp.zeros((rows, 3, local), jnp.float32)
    for j in range(nshort):
        grad_acc = grad_acc + short_filter[j][None] * feats_ext[j : j + rows]
    grad_mixed = grad_acc.astype(jnp.bfloat16)
    short_part = jnp.stack(
        [
            jnp.sum(grad_feats * short_rows[nshort - 1 - j : nshort - 1 - j + rows], axis=0)
            for j in range(nshort)
        ]
    )
    filter_total, short_total = (
        lax.psum(filter_part.astype(jnp.bfloat16), "dp").astype(jnp.float32),
        lax.psum(short_part.astype(jnp.bfloat16), "dp").astype(jnp.float32),
    )
    grad_long = filter_total * scale
    grad_short = short_total * scale
    partial_in = jnp.einsum("sic,dic->sd", grad_mixed, full_w, preferred_element_type=jnp.float32)
    summed_in = lax.psum_scatter(
        partial_in.astype(jnp.bfloat16), ("row", "col"), scatter_dimension=1, tiled=True
    )
    weight_term = (
        jnp.einsum("sd,sic->dic", whole, grad_mixed, preferred_element_type=jnp.float32) * scale
    )
    grad_weight = lax.psum_scatter(
        weight_term.astype(jnp.bfloat16), "dp", scatter_dimension=0, tiled=True
    ).astype(jnp.float32)
    return (mixed, summed_in, grad_weight, grad_long, grad_short)


def solution(mesh):
    placed = (
        P("dp", ("row", "col")),
        P("dp", None, ("row", "col")),
        P(None, None, ("row", "col")),
        P(("row", "col"), None),
        P("dp", ("row", "col")),
    )
    return jax.shard_map(
        per_device,
        mesh=mesh,
        in_specs=placed,
        out_specs=(
            P("dp", ("row", "col")),
            P("dp", ("row", "col")),
            P("dp", None, ("row", "col")),
            P(("row", "col"), None),
            P(None, None, ("row", "col")),
        ),
        check_vma=False,
    )
```

profile of v0, /device:TPU:4, one launch (start us, length us, event | category | flops | bytes accessed | tf_op | source)
XLA Modules:
  0.0 539.4 jit_solution(406576866576352220)
XLA Ops:
  8.7 48.7 %all-gather.3.cloned.1.call-done = bf16[192,4096]{1,0:T(8,128)(2,1)} async-done(((bf16[192,512]{1,0:T(8,128)(2,1)}), bf16[192,4096]{1,0:T(8,128)(2,1)}) %all-gather.3.cloned.1.call-update) | async-done | bytes 1572880 | tf_op jit(solution)/shard_map/all_gather | solution.py:44
  57.4 117.2 %all-gather.5.cloned.1.call-done = bf16[4096,3,512]{2,0,1:T(8,128)(2,1)} async-done(((bf16[128,3,512]{2,0,1:T(8,128)(2,1)}), bf16[4096,3,512]{2,0,1:T(8,128)(2,1)}) %all-gather.5.cloned.1.call-update) | async-done | bytes 12582928 | tf_op jit(solution)/shard_map/all_gather | solution.py:45
  174.6 7.7 %fusion.10 = bf16[192,3,512]{2,0,1:T(8,128)(2,1)S(1)} fusion(bf16[4096,3,512]{2,0,1:T(8,128)(2,1)} %all-gather.5.cloned.1.call-done, bf16[192,4096]{1,0:T(8,128)(2,1)} %all-gather.3.cloned.1.call-done), kind=kOutput, calls=%fused_computation.16 | convolution fusion | flops 2416214016 | bytes 14745600 | tf_op jit(solution)/shard_map/sd,dic->sic/dot_general | solution.py:46
  182.4 2.2 collective-permute-start
  184.7 3.1 tile.8
  187.8 11.6 %tile.9 = bf16[32,98112]{1,0:T(8,128)(2,1)} reshape(bf16[32,192,511]{2,1,0:T(8,128)(2,1)} %tile.8) | data formatting | bytes 12558336 | tf_op jit(solution)/shard_map/tile | solution.py:19
  199.4 5.8 %slice.119 = bf16[32,97920]{1,0:T(8,128)(2,1)} slice(bf16[32,98112]{1,0:T(8,128)(2,1)} %tile.9), slice={[0:32], [0:97920]} | slice | bytes 12533760 | tf_op jit(solution)/shard_map/slice | solution.py:20
  205.3 15.3 %reshape.49 = bf16[32,192,510]{2,1,0:T(8,128)(2,1)} reshape(bf16[32,97920]{1,0:T(8,128)(2,1)} %slice.119) | data formatting | bytes 12533760 | tf_op jit(solution)/shard_map/reshape | solution.py:20
  221.5 1.3 copy-done
  223.1 4.1 fusion.3
  228.1 1.9 fusion.23
  230.0 5.1 collective-permute-start.1
  235.2 3.2 tile.20
  238.3 11.6 %tile.21 = bf16[32,98112]{1,0:T(8,128)(2,1)} reshape(bf16[32,192,511]{2,1,0:T(8,128)(2,1)} %tile.20) | data formatting | bytes 12558336 | tf_op jit(solution)/shard_map/tile | solution.py:19
  249.9 5.8 %slice.122 = bf16[32,97920]{1,0:T(8,128)(2,1)} slice(bf16[32,98112]{1,0:T(8,128)(2,1)} %tile.21), slice={[0:32], [0:97920]} | slice | bytes 12533760 | tf_op jit(solution)/shard_map/slice | solution.py:20
  255.8 15.3 %reshape.52 = bf16[32,192,510]{2,1,0:T(8,128)(2,1)} reshape(bf16[32,97920]{1,0:T(8,128)(2,1)} %slice.122) | data formatting | bytes 12533760 | tf_op jit(solution)/shard_map/reshape | solution.py:20
  272.0 4.2 fusion.1
  277.2 1.4 slice_multiply_fusion.10
  278.7 2.0 collective-permute-start.2
  280.7 1.4 collective-permute-done.2
  283.6 6.6 %multiply_convert_fusion = bf16[3,512,4096]{2,1,0:T(8,128)(2,1)} fusion(bf16[192,3,512]{2,0,1:T(8,128)(2,1)S(1)} %get-tuple-element.29, bf16[192,4096]{1,0:T(8,128)(2,1)S(1)} %copy-done.6), kind=kOutput, calls=%fused_computation | convolution fusion | flops 2428502016 | bytes 14745600 | tf_op jit(solution)/shard_map/sd,sic->dic/dot_general | solution.py:119
  290.2 16.6 %copy.34 = bf16[4096,1536]{1,0:T(8,128)(2,1)} copy(bf16[4096,1536]{0,1:T(8,128)(2,1)} %bitcast.62) | data formatting | bytes 25165824
  307.9 10.0 %fusion = bf16[192,4096]{1,0:T(8,128)(2,1)} fusion(bf16[192,3,512]{2,0,1:T(8,128)(2,1)S(1)} %copy-done.2, bf16[4096,3,512]{2,0,1:T(8,128)(2,1)} %all-gather.5.cloned.1.call-done), kind=kOutput, calls=%fused_computation.2 | convolution fusion | flops 2416705536 | bytes 14745600 | tf_op jit(solution)/shard_map/sic,dic->sd/dot_general | solution.py:114
  318.8 6.9 %fusion.20 = f32[32,192,511]{2,1,0:T(8,128)} fusion(bf16[32,16,192]{2,1,0:T(8,128)(2,1)S(1)} %bitcast.69, bf16[32,16,319]{2,1,0:T(8,128)(2,1)S(1)} %slice.183), kind=kOutput, calls=%fused_computation.33 | convolution fusion | flops 100466688 | bytes 13081600 | tf_op jit(solution)/shard_map/gcs,gcu->gsu/dot_general | solution.py:83
  325.7 13.2 %reshape.55 = f32[32,98112]{1,0:T(8,128)} reshape(f32[32,192,511]{2,1,0:T(8,128)} %fusion.20) | data formatting | bytes 25116672 | tf_op jit(solution)/shard_map/reshape | solution.py:89
  338.8 11.4 %slice.129 = f32[32,97920]{1,0:T(8,128)} slice(f32[32,98112]{1,0:T(8,128)} %reshape.55), slice={[0:32], [0:97920]} | slice | bytes 25067520 | tf_op jit(solution)/shard_map/slice | solution.py:89
  350.3 15.2 %reshape.56 = f32[32,192,510]{2,1,0:T(8,128)} reshape(f32[32,97920]{1,0:T(8,128)} %slice.129) | data formatting | bytes 25067520 | tf_op jit(solution)/shard_map/reshape | solution.py:89
  365.5 4.4 slice_reduce_fusion
  369.9 127.2 %all-reduce.3 = (bf16[32,128]{1,0:T(8,128)(2,1)S(1)}, bf16[3,3,512]{2,1,0:T(4,128)(2,1)S(1)}) all-reduce(bf16[32,128]{1,0:T(8,128)(2,1)S(1)} %slice_reduce_fusion, bf16[3,3,512]{2,1,0:T(4,128)(2,1)S(1)} %pad_maximum_fusion.3), channel_id=1, replica_groups=mesh['dp'=32,'row'=4,'col'=2] {'dp'}, use_global_device_ids=true, to_apply=%region_3.0 | all-reduce | flops 8704 | bytes 34816 | tf_op jit(solution)/shard_map/psum | solution.py:109
  498.4 1.2 copy.35
  499.6 1.1 copy.31
  500.7 32.2 %reduce-scatter.5.cloned.1.call-done = bf16[192,512]{1,0:T(8,128)(2,1)} async-done(((bf16[192,4096]{1,0:T(8,128)(2,1)}), bf16[192,512]{1,0:T(8,128)(2,1)}) %reduce-scatter.5.cloned.1.call-update) | async-done | bytes 196624 | tf_op jit(solution)/shard_map/reduce_scatter | solution.py:115
  (48 shorter events, 10.4 us)
Async XLA Ops:
  7.2 50.3 %all-gather.3.cloned.1.call-start = ((), (), s32[]{:S(2)}) async-start(), calls=%async_computation.2 | async-start | bytes 1769472 | tf_op jit(solution)/shard_map/all_gather | solution.py:44
  7.9 166.7 %all-gather.5.cloned.1.call-start = ((), (), s32[]{:S(2)}) async-start(), calls=%async_computation.3 | async-start | bytes 12976128 | tf_op jit(solution)/shard_map/all_gather | solution.py:45
  8.6 175.9 %copy-start.4 = (bf16[32,128]{1,0:T(8,128)(2,1)S(1)}, bf16[32,128]{1,0:T(8,128)(2,1)}, u32[]{:S(2)}) copy-start(bf16[32,128]{1,0:T(8,128)(2,1)} %param.8) | copy-start | bytes 24580
  8.7 489.7 %reduce-scatter.7.cloned.1.call-start = ((), (), s32[]{:S(2)}) async-start(), calls=%async_computation.5 | async-start | bytes 12976128
  182.4 38.2 %collective-permute-start = (bf16[129,3,512]{2,0,1:T(8,128)(2,1)S(1)}, bf16[129,3,512]{2,0,1:T(8,128)(2,1)S(1)}, u32[]{:S(2)}, u32[]{:S(2)}) collective-permute-start(bf16[129,3,512]{2,0,1:T(8,128)(2,1)S(1)} %slice.112), channel_id=1, source_target_pairs={{0,8},{8,16},{16,24},{24,32},{32,40},{40,48},{48,56},{56,64},{64,7... | collective-permute-start | bytes 1188872 | tf_op jit(solution)/shard_map/ppermute | solution.py:10
  205.3 15.3 %copy-start.5 = (f32[3,3,512]{2,1,0:T(4,128)S(1)}, f32[3,3,512]{2,1,0:T(4,128)}, u32[]{:S(2)}) copy-start(f32[3,3,512]{2,1,0:T(4,128)} %param.7) | copy-start | bytes 55300
  221.5 1.3 copy-start
  223.1 5.1 copy-start.3
  230.0 41.0 %collective-permute-start.1 = (bf16[127,512]{1,0:T(8,128)(2,1)S(1)}, bf16[127,512]{1,0:T(8,128)(2,1)S(1)}, u32[]{:S(2)}, u32[]{:S(2)}) collective-permute-start(bf16[127,512]{1,0:T(8,128)(2,1)S(1)} %slice.121), channel_id=1, source_target_pairs={{8,0},{16,8},{24,16},{32,24},{40,32},{48,40},{56,48},{64,56},{72,6... | collective-permute-start | bytes 390152 | tf_op jit(solution)/shard_map/ppermute | solution.py:10
  278.7 3.4 collective-permute-start.2
  282.2 1.4 copy-start.6
  283.0 7.2 %copy-start.1 = (bf16[192,3,512]{2,0,1:T(8,128)(2,1)}, bf16[192,3,512]{2,0,1:T(8,128)(2,1)S(1)}, u32[]{:S(2)}) copy-start(bf16[192,3,512]{2,0,1:T(8,128)(2,1)S(1)} %get-tuple-element.29) | copy-start | bytes 1769476
  306.8 1.1 copy-start.2
  306.9 226.0 %reduce-scatter.5.cloned.1.call-start = ((), (), s32[]{:S(2)}) async-start(), calls=%async_computation.4 | async-start | bytes 1769472 | tf_op jit(solution)/shard_map/reduce_scatter | solution.py:115
Sparse Core Ops, SparseCore 0:
  9.8 47.6 all-gather.2
  60.2 114.3 all-gather.4
  307.0 175.7 reduce-scatter.6
  485.8 47.0 reduce-scatter.4
where the time goes:
time: 540 us; the launch traced here: 539 us
  waiting for transfers between devices  201 us (37%)
  local copies, waits for them, and re-layouts  137 us (25%)
  blocking collectives  127 us (24%)
  matrix products  39.5 us (7%)
  between operations  14 us (3%)
  other arithmetic  10.9 us (2%)
  starting transfers between devices  9.64 us (2%)
    psum x1, blocking collectives, per_device(): lax.psum(filter_part.astype(jnp.bfloat16), 'dp').astype(jnp.float32)  127 us
    all_gather x1, waiting for transfers between devices, per_device(): full_w = lax.all_gather(in_weight, 'dp', axis=0, tiled=True)  117 us
    all_gather x1, waiting for transfers between devices, per_device(): whole = lax.all_gather(tokens, ('row', 'col'), axis=1, tiled=True)  48.7 us
    reduce_scatter x1, waiting for transfers between devices, per_device(): lax.psum_scatter(partial_in.astype(jnp.bfloat16), ('row', 'col'), scatter...  32.2 us
    reshape x2, local copies, waits for them, and re-layouts, toeplitz(): skewed = tiled[:, :rows * (width - 1)].reshape(groups, rows, width - 1)  30.6 us
    another operation x4, local copies, waits for them, and re-layouts, toeplitz(): tiled = jnp.tile(seed_row, (1, rows))  29.5 us
    reshape x2, local copies, waits for them, and re-layouts, per_device(): pairs.reshape(ngroups, rows * width)[:, :rows * (width - 1)]  28.4 us
    unnamed x19, local copies, waits for them, and re-layouts  22.2 us
  transfers between devices with their start and end apart: 7, of which 4 were waited for; matrix products, arithmetic and copies ran while one was open for 25% of the time, Pallas kernels for 0%

commit v1 on v0

--- a/solution.py
+++ b/solution.py
@@ -41,7 +41,8 @@
     margin = ntaps - 1
     span = rows + margin
     scale = float(rows * lax.axis_size("dp")) ** (-0.5)
-    whole = lax.all_gather(tokens, ("row", "col"), axis=1, tiled=True)
+    repeated = jnp.stack([tokens] * lax.axis_size(("row", "col")))
+    whole = jnp.concatenate(lax.all_to_all(repeated, ("row", "col"), 0, 0), axis=1)
     full_w = lax.all_gather(in_weight, "dp", axis=0, tiled=True)
     mixed_in = jnp.einsum("sd,dic->sic", whole, full_w, preferred_element_type=jnp.float32).astype(
         jnp.bfloat16

time: 540 us -> 498 us (0.922)
  waiting for transfers between devices: 201 us -> 124 us
  blocking collectives: 127 us -> 158 us
    all_gather x1 -> x0, waiting for transfers between devices: 48.7 us -> none  [per_device(): whole = lax.all_gather(tokens, ('row', 'col'), axis=1, tiled=True)]
    all_to_all x0 -> x1, blocking collectives: none -> 30.6 us  [per_device(): lax.all_to_all(repeated, ('row', 'col'), 0, 0)]
    all_gather x1, waiting for transfers between devices: 117 us -> 89.6 us  [per_device(): full_w = lax.all_gather(in_weight, 'dp', axis=0, tiled=True)]
  transfers between devices with their start and end apart: 7 -> 6, of which waited for: 4 -> 3; matrix products, arithmetic and copies ran while one was open for 25% -> 28% of each run, Pallas kernels for 0% -> 0%
where the time goes in v1:
time: 498 us; the launch traced here: 497 us
  blocking collectives  158 us (32%)
  local copies, waits for them, and re-layouts  141 us (28%)
  waiting for transfers between devices  124 us (25%)
  matrix products  39.2 us (8%)
  between operations  14 us (3%)
  other arithmetic  10.9 us (2%)
  starting transfers between devices  9.61 us (2%)
    psum x1, blocking collectives, per_device(): lax.psum(filter_part.astype(jnp.bfloat16), 'dp').astype(jnp.float32)  127 us
    all_gather x1, waiting for transfers between devices, per_device(): full_w = lax.all_gather(in_weight, 'dp', axis=0, tiled=True)  89.6 us
    reduce_scatter x1, waiting for transfers between devices, per_device(): lax.psum_scatter(partial_in.astype(jnp.bfloat16), ('row', 'col'), scatter...  32.5 us
    all_to_all x1, blocking collectives, per_device(): lax.all_to_all(repeated, ('row', 'col'), 0, 0)  30.6 us
    reshape x2, local copies, waits for them, and re-layouts, toeplitz(): skewed = tiled[:, :rows * (width - 1)].reshape(groups, rows, width - 1)  30.6 us
    another operation x4, local copies, waits for them, and re-layouts, toeplitz(): tiled = jnp.tile(seed_row, (1, rows))  29.5 us
    reshape x2, local copies, waits for them, and re-layouts, per_device(): pairs.reshape(ngroups, rows * width)[:, :rows * (width - 1)]  28.3 us
    unnamed x19, local copies, waits for them, and re-layouts  22.3 us
  transfers between devices with their start and end apart: 6, of which 3 were waited for; matrix products, arithmetic and copies ran while one was open for 28% of the time, Pallas kernels for 0%

profile of v1, /device:TPU:4, one launch (start us, length us, event | category | flops | bytes accessed | tf_op | source)
XLA Modules:
  0.0 496.8 jit_solution(17393841461693125012)
XLA Ops:
  9.0 30.6 %all_to_all.5 = bf16[8,192,512]{2,1,0:T(8,128)(2,1)S(1)} all-to-all(bf16[8,192,512]{2,1,0:T(8,128)(2,1)S(1)} %stack.35), channel_id=1, replica_groups=mesh['dp'=32,'row'=4,'col'=2] {'row','col'}, dimensions={0} | all-to-all | bytes 3145728 | tf_op jit(solution)/shard_map/all_to_all | solution.py:45
  40.5 2.1 reshape.67
  42.6 89.6 %all-gather.2.cloned.1.call-done = bf16[4096,3,512]{2,0,1:T(8,128)(2,1)} async-done(((bf16[128,3,512]{2,0,1:T(8,128)(2,1)}), bf16[4096,3,512]{2,0,1:T(8,128)(2,1)}) %all-gather.2.cloned.1.call-update) | async-done | bytes 12582928 | tf_op jit(solution)/shard_map/all_gather | solution.py:46
  132.2 7.7 %convolution_convert_fusion = bf16[192,3,512]{2,0,1:T(8,128)(2,1)S(1)} fusion(bf16[192,4096,1]{1,0,2:T(8,128)(2,1)} %reshape.67, bf16[4096,3,512]{2,0,1:T(8,128)(2,1)} %all-gather.2.cloned.1.call-done), kind=kOutput, calls=%fused_computation.13 | convolution fusion | flops 2416214016 | bytes 14745600 | tf_op jit(solution)/shard_map/sd,dic->sic/dot_general | solution.py:47
  139.9 2.2 collective-permute-start
  142.2 3.2 tile.8
  145.4 11.6 %tile.9 = bf16[32,98112]{1,0:T(8,128)(2,1)} reshape(bf16[32,192,511]{2,1,0:T(8,128)(2,1)} %tile.8) | data formatting | bytes 12558336 | tf_op jit(solution)/shard_map/tile | solution.py:19
  157.0 5.8 %slice.119 = bf16[32,97920]{1,0:T(8,128)(2,1)} slice(bf16[32,98112]{1,0:T(8,128)(2,1)} %tile.9), slice={[0:32], [0:97920]} | slice | bytes 12533760 | tf_op jit(solution)/shard_map/slice | solution.py:20
  162.8 15.3 %reshape.59 = bf16[32,192,510]{2,1,0:T(8,128)(2,1)} reshape(bf16[32,97920]{1,0:T(8,128)(2,1)} %slice.119) | data formatting | bytes 12533760 | tf_op jit(solution)/shard_map/reshape | solution.py:20
  179.0 1.3 copy-done
  180.6 4.1 fusion.3
  185.7 1.9 fusion.17
  187.6 5.1 %collective-permute-start.1 = (bf16[127,512]{1,0:T(8,128)(2,1)S(1)}, bf16[127,512]{1,0:T(8,128)(2,1)S(1)}, u32[]{:S(2)}, u32[]{:S(2)}) collective-permute-start(bf16[127,512]{1,0:T(8,128)(2,1)S(1)} %slice.121), channel_id=1, source_target_pairs={{8,0},{16,8},{24,16},{32,24},{40,32},{48,40},{56,48},{64,56},{72,6... | collective-permute-start | bytes 390152 | tf_op jit(solution)/shard_map/ppermute | solution.py:10
  192.7 3.2 tile.20
  195.9 11.6 %tile.21 = bf16[32,98112]{1,0:T(8,128)(2,1)} reshape(bf16[32,192,511]{2,1,0:T(8,128)(2,1)} %tile.20) | data formatting | bytes 12558336 | tf_op jit(solution)/shard_map/tile | solution.py:19
  207.5 5.8 %slice.122 = bf16[32,97920]{1,0:T(8,128)(2,1)} slice(bf16[32,98112]{1,0:T(8,128)(2,1)} %tile.21), slice={[0:32], [0:97920]} | slice | bytes 12533760 | tf_op jit(solution)/shard_map/slice | solution.py:20
  213.3 15.3 %reshape.62 = bf16[32,192,510]{2,1,0:T(8,128)(2,1)} reshape(bf16[32,97920]{1,0:T(8,128)(2,1)} %slice.122) | data formatting | bytes 12533760 | tf_op jit(solution)/shard_map/reshape | solution.py:20
  229.6 4.2 fusion.1
  234.7 1.4 slice_multiply_fusion.10
  236.2 2.0 collective-permute-start.2
  238.2 1.4 collective-permute-done.2
  241.1 6.4 %multiply_convert_fusion = bf16[3,512,4096]{2,1,0:T(8,128)(2,1)} fusion(bf16[192,3,512]{2,0,1:T(8,128)(2,1)S(1)} %get-tuple-element.29, bf16[192,4096,1]{1,0,2:T(8,128)(2,1)S(1)} %copy-done.1), kind=kOutput, calls=%fused_computation | convolution fusion | flops 2428502016 | bytes 14745600 | tf_op jit(solution)/shard_map/sd,sic->dic/dot_general | solution.py:120
  247.6 16.7 %copy.35 = bf16[4096,1536]{1,0:T(8,128)(2,1)} copy(bf16[4096,1536]{0,1:T(8,128)(2,1)} %bitcast.58) | data formatting | bytes 25165824
  265.3 10.0 %fusion = bf16[192,4096]{1,0:T(8,128)(2,1)} fusion(bf16[192,3,512]{2,0,1:T(8,128)(2,1)S(1)} %copy-done.3, bf16[4096,3,512]{2,0,1:T(8,128)(2,1)} %all-gather.2.cloned.1.call-done), kind=kOutput, calls=%fused_computation.2 | convolution fusion | flops 2416705536 | bytes 14745600 | tf_op jit(solution)/shard_map/sic,dic->sd/dot_general | solution.py:115
  276.2 6.9 %fusion.14 = f32[32,192,511]{2,1,0:T(8,128)} fusion(bf16[32,16,192]{2,1,0:T(8,128)(2,1)S(1)} %bitcast.66, bf16[32,16,319]{2,1,0:T(8,128)(2,1)S(1)} %slice.183), kind=kOutput, calls=%fused_computation.30 | convolution fusion | flops 100466688 | bytes 13081600 | tf_op jit(solution)/shard_map/gcs,gcu->gsu/dot_general | solution.py:84
  283.1 13.2 %reshape.65 = f32[32,98112]{1,0:T(8,128)} reshape(f32[32,192,511]{2,1,0:T(8,128)} %fusion.14) | data formatting | bytes 25116672 | tf_op jit(solution)/shard_map/reshape | solution.py:90
  296.2 11.4 %slice.129 = f32[32,97920]{1,0:T(8,128)} slice(f32[32,98112]{1,0:T(8,128)} %reshape.65), slice={[0:32], [0:97920]} | slice | bytes 25067520 | tf_op jit(solution)/shard_map/slice | solution.py:90
  307.7 15.2 %reshape.66 = f32[32,192,510]{2,1,0:T(8,128)} reshape(f32[32,97920]{1,0:T(8,128)} %slice.129) | data formatting | bytes 25067520 | tf_op jit(solution)/shard_map/reshape | solution.py:90
  322.9 4.4 slice_reduce_fusion
  327.3 127.0 %all-reduce.3 = (bf16[32,128]{1,0:T(8,128)(2,1)S(1)}, bf16[3,3,512]{2,1,0:T(4,128)(2,1)S(1)}) all-reduce(bf16[32,128]{1,0:T(8,128)(2,1)S(1)} %slice_reduce_fusion, bf16[3,3,512]{2,1,0:T(4,128)(2,1)S(1)} %pad_maximum_fusion.3), channel_id=1, replica_groups=mesh['dp'=32,'row'=4,'col'=2] {'dp'}, use_global_device_ids=true, to_apply=%region_3.0 | all-reduce | flops 8704 | bytes 34816 | tf_op jit(solution)/shard_map/psum | solution.py:110
  455.5 1.2 copy.36
  457.8 32.5 %reduce-scatter.5.cloned.1.call-done = bf16[192,512]{1,0:T(8,128)(2,1)} async-done(((bf16[192,4096]{1,0:T(8,128)(2,1)}), bf16[192,512]{1,0:T(8,128)(2,1)}) %reduce-scatter.5.cloned.1.call-update) | async-done | bytes 196624 | tf_op jit(solution)/shard_map/reduce_scatter | solution.py:116
  (49 shorter events, 12.7 us)
Async XLA Ops:
  7.2 125.0 %all-gather.2.cloned.1.call-start = ((), (), s32[]{:S(2)}) async-start(), calls=%async_computation.3 | async-start | bytes 12976128 | tf_op jit(solution)/shard_map/all_gather | solution.py:46
  7.9 447.6 %reduce-scatter.7.cloned.1.call-start = ((), (), s32[]{:S(2)}) async-start(), calls=%async_computation.5 | async-start | bytes 12976128
  42.6 99.5 %copy-start.5 = (bf16[32,128]{1,0:T(8,128)(2,1)S(1)}, bf16[32,128]{1,0:T(8,128)(2,1)}, u32[]{:S(2)}) copy-start(bf16[32,128]{1,0:T(8,128)(2,1)} %param.8) | copy-start | bytes 24580
  139.9 38.2 %collective-permute-start = (bf16[129,3,512]{2,0,1:T(8,128)(2,1)S(1)}, bf16[129,3,512]{2,0,1:T(8,128)(2,1)S(1)}, u32[]{:S(2)}, u32[]{:S(2)}) collective-permute-start(bf16[129,3,512]{2,0,1:T(8,128)(2,1)S(1)} %slice.112), channel_id=1, source_target_pairs={{0,8},{8,16},{16,24},{24,32},{32,40},{40,48},{48,56},{56,64},{64,7... | collective-permute-start | bytes 1188872 | tf_op jit(solution)/shard_map/ppermute | solution.py:10
  162.8 15.3 %copy-start.6 = (f32[3,3,512]{2,1,0:T(4,128)S(1)}, f32[3,3,512]{2,1,0:T(4,128)}, u32[]{:S(2)}) copy-start(f32[3,3,512]{2,1,0:T(4,128)} %param.7) | copy-start | bytes 55300
  179.0 1.3 copy-start
  180.6 5.1 %copy-start.4 = (bf16[192,512]{1,0:T(8,128)(2,1)S(1)}, bf16[192,512]{1,0:T(8,128)(2,1)}, u32[]{:S(2)}) copy-start(bf16[192,512]{1,0:T(8,128)(2,1)} %param.9) | copy-start | bytes 589828
  187.6 41.0 %collective-permute-start.1 = (bf16[127,512]{1,0:T(8,128)(2,1)S(1)}, bf16[127,512]{1,0:T(8,128)(2,1)S(1)}, u32[]{:S(2)}, u32[]{:S(2)}) collective-permute-start(bf16[127,512]{1,0:T(8,128)(2,1)S(1)} %slice.121), channel_id=1, source_target_pairs={{8,0},{16,8},{24,16},{32,24},{40,32},{48,40},{56,48},{64,56},{72,6... | collective-permute-start | bytes 390152 | tf_op jit(solution)/shard_map/ppermute | solution.py:10
  236.2 3.4 collective-permute-start.2
  239.7 1.4 copy-start.1
  240.6 7.0 %copy-start.2 = (bf16[192,3,512]{2,0,1:T(8,128)(2,1)}, bf16[192,3,512]{2,0,1:T(8,128)(2,1)S(1)}, u32[]{:S(2)}) copy-start(bf16[192,3,512]{2,0,1:T(8,128)(2,1)S(1)} %get-tuple-element.29) | copy-start | bytes 1769476
  264.3 1.1 copy-start.3
  264.3 226.0 %reduce-scatter.5.cloned.1.call-start = ((), (), s32[]{:S(2)}) async-start(), calls=%async_computation.4 | async-start | bytes 1769472 | tf_op jit(solution)/shard_map/reduce_scatter | solution.py:116
Sparse Core Ops, SparseCore 0:
  10.8 121.3 all-gather.1
  264.4 175.4 reduce-scatter.6
  443.0 47.2 reduce-scatter.4
